TPU v7x, 32 devices: a whole 2x2x4 slice. The times are simulated.
32 devices in a mesh: az: 4 (over z), rad: 2 (over x), ax: 4 (over y, core).
Axes of the slice: x: 2, y: 2, z: 4, core: 2. Of those that a mesh axis runs over, the one named last changes fastest.
Arguments:
- cycle: float32 [4, 5, 512, 4096], P(None, None, ('rad', 'ax'), 'az'), may hold values from -6 to 6
- field: float32 [5, 64, 8, 4096], P(None, 'rad', 'ax', 'az'), may hold values from -6 to 6
- shift: int32 [1], replicated, may hold values from 0 to 4095
- owner: int32 [64, 8], P('rad', 'ax'), may hold values 0 or 1
Outputs:
- field_next: float32 [5, 64, 8, 4096], P(None, 'rad', 'ax', 'az')
- shifted_cycle: float32 [4, 5, 512, 4096], P(None, None, ('rad', 'ax'), 'az')
All inputs are finite; a program needn't handle non-finite values. No bound on the sum of `owner` on one device may be relied on, other than what follows from the above.
Results may differ from a plain program's by a relative error of at most 0.00007.
Values sent between devices are 32-bit elements; how exact they have to be, the bound alone decides.
A program may use at most 192 MiB of HBM per device.

v0:
```python
import math
import jax
import jax.numpy as jnp
from jax import lax
from jax.sharding import PartitionSpec as P

KR = 8
LAYER_WEIGHTS = (0.4, 0.3, 0.2, 0.1)
AXIAL_SPEEDS = (0.35, 0.2, 0.3, 0.25, 0.4)
DIFFUSION = 0.15
SWIRL_SPEED = 0.1


def padded(array, sides, width):
    for axis, dim in sides:
        devices, length = (lax.axis_size(axis), array.shape[dim])
        up = [(i, (i + 1) % devices) for i in range(devices - 1)]
        down = [(j, i) for i, j in up]
        last = lax.slice_in_dim(array, length - width, length, axis=dim)
        leading = lax.slice_in_dim(array, 0, width, axis=dim)
        before = lax.ppermute(last, axis, up)
        after = lax.ppermute(leading, axis, down)
        array = jnp.concatenate([before, array, after], axis=dim)
    return array


def turn_table(first, second, modulus):
    product = jnp.remainder(first[:, None] * second[None, :], modulus).astype(jnp.float32)
    angle = product * (2.0 * math.pi / modulus)
    return (jnp.cos(angle), jnp.sin(angle))


def spectral_shift(rows, shift_value):
    count, length = rows.shape
    half_bits = (length.bit_length() - 1) // 2
    outer = 2**half_bits
    inner = length // outer
    hp = lax.Precision.HIGHEST
    outer_index = jnp.arange(outer, dtype=jnp.int32)
    inner_index = jnp.arange(inner, dtype=jnp.int32)
    cos_outer, sin_outer = turn_table(outer_index, outer_index, outer)
    cos_inner, sin_inner = turn_table(inner_index, inner_index, inner)
    cos_twist, sin_twist = turn_table(outer_index, inner_index, length)
    grid = rows.reshape(count, outer, inner)
    section_re = jnp.einsum("bpq,pk->bkq", grid, cos_outer, precision=hp)
    section_im = -jnp.einsum("bpq,pk->bkq", grid, sin_outer, precision=hp)
    twist_re = section_re * cos_twist + section_im * sin_twist
    twist_im = section_im * cos_twist - section_re * sin_twist
    spec_re = jnp.einsum("bkq,qm->bkm", twist_re, cos_inner, precision=hp) + jnp.einsum(
        "bkq,qm->bkm", twist_im, sin_inner, precision=hp
    )
    spec_im = jnp.einsum("bkq,qm->bkm", twist_im, cos_inner, precision=hp) - jnp.einsum(
        "bkq,qm->bkm", twist_re, sin_inner, precision=hp
    )
    wave = outer_index[:, None] + outer * inner_index[None, :]
    folded = jnp.minimum(wave, length - wave)
    filt = (3 * folded < length).astype(jnp.float32)
    phase = jnp.remainder(wave * shift_value, length).astype(jnp.float32) * (2.0 * math.pi / length)
    gain_re = filt * jnp.cos(phase)
    gain_im = -filt * jnp.sin(phase)
    mixed_re = spec_re * gain_re - spec_im * gain_im
    mixed_im = spec_re * gain_im + spec_im * gain_re
    back_re = jnp.einsum("bkm,qm->bkq", mixed_re, cos_inner, precision=hp) - jnp.einsum(
        "bkm,qm->bkq", mixed_im, sin_inner, precision=hp
    )
    back_im = jnp.einsum("bkm,qm->bkq", mixed_im, cos_inner, precision=hp) + jnp.einsum(
        "bkm,qm->bkq", mixed_re, sin_inner, precision=hp
    )
    turn_re = back_re * cos_twist - back_im * sin_twist
    turn_im = back_im * cos_twist + back_re * sin_twist
    result = jnp.einsum("bkq,pk->bpq", turn_re, cos_outer, precision=hp) - jnp.einsum(
        "bkq,pk->bpq", turn_im, sin_outer, precision=hp
    )
    return (result / length).reshape(count, length)


def on_device(cycle, field, shift, owner):
    layers, variables, radial, sector = cycle.shape
    stacked = cycle.reshape(layers * variables, radial, sector)
    shift_value = shift[0]
    piece = lax.all_to_all(stacked, "az", split_axis=1, concat_axis=2, tiled=True)
    moved = spectral_shift(piece.reshape(-1, piece.shape[2]), shift_value).reshape(piece.shape)
    shifted_flat = lax.all_to_all(moved, "az", split_axis=2, concat_axis=1, tiled=True)
    shifted_cycle = shifted_flat.reshape(layers, variables, radial, sector)
    weights = jnp.array(LAYER_WEIGHTS, jnp.float32)
    depth, count, rows, width = shifted_cycle.shape
    grouped = shifted_cycle.reshape(depth, count, rows // KR, KR, width)
    ghost = lax.all_gather(
        jnp.einsum("l,lvrkt->vrt", weights, grouped, precision=lax.Precision.HIGHEST) / KR,
        "ax",
        axis=1,
        tiled=True,
    )
    mask = owner.astype(jnp.float32)[None, :, :, None]
    speeds = jnp.array(AXIAL_SPEEDS, jnp.float32)[:, None, None, None]
    at_inlet = lax.axis_index("ax") == 0

    def rates(state):
        radial_pad = padded(state, (("rad", 1),), 1)
        axial_pad = padded(state, (("ax", 2),), 1)
        lower = jnp.where(at_inlet, ghost, axial_pad[:, :, 0])
        outward = radial_pad[:, 2:]
        inward = radial_pad[:, :-2]
        above = axial_pad[:, :, 2:]
        below = jnp.concatenate([lower[:, :, None], axial_pad[:, :, 1:-2]], axis=2)
        return mask * (
            DIFFUSION * (outward + inward + above + below - 4.0 * state)
            - 0.5 * speeds * (above - below)
            - 0.5 * SWIRL_SPEED * (outward - inward)
        )

    first = rates(field)
    second = rates(field + 0.5 * first)
    third = rates(field + 0.5 * second)
    fourth = rates(field + third)
    field_next = field + (first + 2.0 * second + 2.0 * third + fourth) / 6.0
    return (field_next, shifted_cycle)


def solution(mesh):
    in_specs = (P(None, None, ("rad", "ax"), "az"), P(None, "rad", "ax", "az"), P(), P("rad", "ax"))
    out_specs = (P(None, "rad", "ax", "az"), P(None, None, ("rad", "ax"), "az"))
    return jax.shard_map(
        on_device, mesh=mesh, in_specs=in_specs, out_specs=out_specs, check_vma=False
    )
```

profile of v0, /device:TPU:1, one launch (start us, length us, event | category | flops | bytes accessed | tf_op | source)
XLA Modules:
  0.0 716.4 jit_solution(15796967327889109579)
XLA Ops:
  0.6 8.2 %copy.187 = f32[20,64,1024]{2,0,1:T(8,128)} copy(f32[20,64,1024]{2,1,0:T(8,128)} %bitcast.97) | data formatting | bytes 10485760 | tf_op jit(solution)/shard_map/reshape | solution.py:79
  8.8 5.6 all-to-all-start
  15.6 137.3 %all-to-all-done = f32[20,64,1024]{2,0,1:T(8,128)} async-done(((f32[20,64,1024]{2,0,1:T(8,128)}), f32[20,64,1024]{2,0,1:T(8,128)}, u32[]{:S(2)}, u32[]{:S(2)}) %all-to-all-start) | async-done | bytes 5242912 | tf_op jit(solution)/shard_map/all_to_all | solution.py:81
  152.9 8.5 %copy.189 = f32[20,16,4,1024]{3,2,1,0:T(4,128)} copy(f32[20,16,4,1024]{3,0,1,2:T(8,128)} %bitcast.5) | data formatting | bytes 10485760 | tf_op jit(solution)/shard_map/all_to_all | solution.py:81
  161.4 9.6 %reshape_reshape.9 = f32[320,64,64]{2,1,0:T(8,128)} reshape(f32[20,16,4,1024]{3,2,1,0:T(4,128)} %copy.189) | data formatting | bytes 10485760 | tf_op jit(solution)/shard_map/reshape;reshape | solution.py:44
  171.1 11.8 %copy.191 = f32[320,64,64]{0,1,2:T(8,128)} copy(f32[320,64,64]{2,1,0:T(8,128)} %reshape_reshape.9) | data formatting | bytes 10485760 | tf_op jit(solution)/shard_map/reshape;reshape | solution.py:44
  182.9 8.7 %fusion.44 = f32[64,320,64]{1,0,2:T(8,128)S(1)} fusion(f32[320,64,64]{0,1,2:T(8,128)} %copy.191), kind=kOutput, calls=%fused_computation.85 | convolution fusion | flops 1006690304 | bytes 10485760 | tf_op jit(solution)/shard_map/bpq,pk->bkq/dot_general | solution.py:46
  191.6 7.6 %add_bitcast_fusion = (f32[320,64,64]{0,1,2:T(8,128)S(1)}, f32[320,64,64]{0,1,2:T(8,128)S(1)}) fusion(f32[64,320,64]{1,0,2:T(8,128)S(1)} %fusion.44, f32[64,64]{0,1:T(8,128)S(1)} %copy.195, f32[64,64]{0,1:T(8,128)S(1)} %copy.192, f32[320,64,64]{0,1,2:T(8,128)S(1)} %copy-done.2), kind=kOutput, calls=%fused_computation.10 | convolution fusion | flops 1015865344 | bytes 21004288 | tf_op jit(solution)/shard_map/bpq,pk->bkq/dot_general | solution.py:45
  199.2 14.0 %fusion.10 = f32[320,64,64]{0,2,1:T(8,128)} fusion(f32[320,64,64]{0,1,2:T(8,128)S(1)} %get-tuple-element.16), kind=kOutput, calls=%fused_computation.17 | convolution fusion | flops 1006690304 | bytes 10485760 | tf_op jit(solution)/shard_map/bkq,qm->bkm/dot_general | solution.py:49
  213.2 13.2 %fusion.8 = f32[320,64,64]{0,2,1:T(8,128)} fusion(f32[320,64,64]{0,1,2:T(8,128)S(1)} %get-tuple-element.16), kind=kOutput, calls=%fused_computation.15 | convolution fusion | flops 1006690304 | bytes 10485760 | tf_op jit(solution)/shard_map/bkq,qm->bkm/dot_general | solution.py:52
  226.4 13.3 %fusion.6 = f32[320,64,64]{0,2,1:T(8,128)} fusion(f32[320,64,64]{0,1,2:T(8,128)S(1)} %get-tuple-element.17), kind=kOutput, calls=%fused_computation.13 | convolution fusion | flops 1006690304 | bytes 10485760 | tf_op jit(solution)/shard_map/bkq,qm->bkm/dot_general | solution.py:49
  239.7 19.1 %multiply_subtract_fusion.1 = (f32[320,64,64]{0,2,1:T(8,128)}, f32[320,64,64]{0,2,1:T(8,128)S(1)}) fusion(f32[64,64]{1,0:T(8,128)S(1)} %get-tuple-element.35, f32[64,64]{1,0:T(8,128)S(1)} %get-tuple-element.34, f32[320,64,64]{0,2,1:T(8,128)} %fusion.8, f32[320,64,64]{0,2,1:T(8,128)} %fusion.10, f32[320,64,64]{0,2,1:T(8,128)} %fusion.6, ...), kind=kOutput, calls=%fused_computation.8 | convolution fusion | flops 1017176064 | bytes 31490048 | tf_op jit(solution)/shard_map/bkq,qm->bkm/dot_general | solution.py:52
  258.9 10.3 %fusion.38 = f32[320,64,64]{0,2,1:T(8,128)} fusion(f32[320,64,64]{0,2,1:T(8,128)} %get-tuple-element.14), kind=kOutput, calls=%fused_computation.79 | convolution fusion | flops 1006690304 | bytes 10485760 | tf_op jit(solution)/shard_map/bkm,qm->bkq/dot_general | solution.py:66
  269.2 7.8 %fusion.53 = f32[320,64,64]{0,2,1:T(8,128)} fusion(f32[320,64,64]{0,2,1:T(8,128)S(1)} %copy-done), kind=kOutput, calls=%fused_computation.94 | convolution fusion | flops 1006690304 | bytes 10485760 | tf_op jit(solution)/shard_map/bkm,qm->bkq/dot_general | solution.py:63
  277.0 7.9 %fusion.40 = f32[320,64,64]{0,2,1:T(8,128)} fusion(f32[320,64,64]{0,2,1:T(8,128)S(1)} %get-tuple-element.15), kind=kOutput, calls=%fused_computation.81 | convolution fusion | flops 1006690304 | bytes 10485760 | tf_op jit(solution)/shard_map/bkm,qm->bkq/dot_general | solution.py:63
  284.9 15.2 %multiply_subtract_fusion = (f32[320,64,64]{0,2,1:T(8,128)}, f32[320,64,64]{0,2,1:T(8,128)}) fusion(f32[64,64]{1,0:T(8,128)S(1)} %get-tuple-element.36, f32[64,64]{1,0:T(8,128)S(1)} %get-tuple-element.37, f32[320,64,64]{0,2,1:T(8,128)} %fusion.38, f32[320,64,64]{0,2,1:T(8,128)} %fusion.53, f32[320,64,64]{0,2,1:T(8,128)} %fusion.40, ...), kind=kOutput, calls=%fused_computation.6 | convolution fusion | flops 1017176064 | bytes 31490048 | tf_op jit(solution)/shard_map/bkm,qm->bkq/dot_general | solution.py:66
  300.1 12.4 %fusion = f32[64,320,64]{1,0,2:T(8,128)S(1)} fusion(f32[320,64,64]{0,2,1:T(8,128)} %get-tuple-element.13), kind=kOutput, calls=%fused_computation | convolution fusion | flops 1006690304 | bytes 10485760 | tf_op jit(solution)/shard_map/bkq,pk->bpq/dot_general | solution.py:71
  312.5 11.2 %multiply_bitcast_fusion = f32[320,64,64]{0,1,2:T(8,128)} fusion(f32[64,320,64]{1,0,2:T(8,128)S(1)} %fusion, f32[320,64,64]{0,2,1:T(8,128)S(1)} %copy-done.3), kind=kOutput, calls=%fused_computation.4 | convolution fusion | flops 1009311744 | bytes 15728640 | tf_op jit(solution)/shard_map/bkq,pk->bpq/dot_general | solution.py:71
  323.7 12.6 %copy.206 = f32[320,64,64]{2,1,0:T(8,128)} copy(f32[320,64,64]{0,1,2:T(8,128)} %multiply_bitcast_fusion) | data formatting | bytes 10485760 | tf_op jit(solution)/shard_map/div | solution.py:74
  336.2 9.7 %reshape_reshape.10 = f32[20,16,4096]{2,1,0:T(8,128)} reshape(f32[320,64,64]{2,1,0:T(8,128)} %copy.206) | data formatting | bytes 10485760 | tf_op jit(solution)/shard_map/reshape;reshape | solution.py:82
  346.0 18.7 %copy.207 = f32[20,16,4096]{0,1,2:T(8,128)} copy(f32[20,16,4096]{2,1,0:T(8,128)} %reshape_reshape.10) | data formatting | bytes 10485760 | tf_op jit(solution)/shard_map/reshape;reshape | solution.py:82
  364.7 56.1 %reshape.131 = f32[4,1,327680]{2,1,0:T(1,128)} reshape(f32[4096,16,20]{2,1,0:T(8,128)} %bitcast.92) | data formatting | bytes 10485760
  420.9 5.2 all-to-all-start.1
  427.5 4.3 collective-permute-start.3
  439.1 102.1 %all-to-all-done.1 = f32[4,1,327680]{2,1,0:T(1,128)} async-done(((f32[4,1,327680]{2,1,0:T(1,128)}), f32[4,1,327680]{2,1,0:T(1,128)}, u32[]{:S(2)}, u32[]{:S(2)}) %all-to-all-start.1) | async-done | bytes 5242912 | tf_op jit(solution)/shard_map/all_to_all | solution.py:83
  541.8 18.3 %reduce = f32[4,327680]{1,0:T(4,128)} reduce(f32[4,1,327680]{2,1,0:T(1,128)} %all-to-all-done.1, f32[]{:T(128)} %broadcast.363), dimensions={1}, to_apply=%all_to_all.25.reduce_sub_computation | reduce | bytes 10485764 | tf_op jit(solution)/shard_map/all_to_all | solution.py:83
  560.1 52.9 %reshape.132 = f32[4096,16,20]{2,1,0:T(8,128)} reshape(f32[4,327680]{1,0:T(4,128)} %reduce) | data formatting | bytes 10485760
  613.0 22.4 %copy.234 = f32[20,16,4,1024]{3,2,1,0:T(4,128)} copy(f32[20,16,4,1024]{0,1,3,2:T(8,128)} %bitcast.93) | data formatting | bytes 10485760 | tf_op jit(solution)/shard_map/all_to_all | solution.py:83
  635.4 9.2 %copy.209 = f32[20,4,16,1024]{3,2,1,0:T(8,128)} copy(f32[20,4,16,1024]{3,1,2,0:T(4,128)} %bitcast.94) | data formatting | bytes 10485760 | tf_op jit(solution)/shard_map/all_to_all | solution.py:83
  644.6 4.6 reduce_sum.9
  651.9 9.0 %all_gather.3 = f32[5,32,1024]{2,1,0:T(8,128)S(1)} all-gather(f32[5,8,1024]{2,1,0:T(8,128)S(1)} %bitcast_multiply_fusion), channel_id=1, replica_groups=mesh['az'=4,'rad'=2,'ax'=4] {'ax'}, dimensions={1}, use_global_device_ids=true | all-gather | bytes 819200 | tf_op jit(solution)/shard_map/all_gather | solution.py:88
  708.6 5.5 multiply_add_fusion.2
  (75 shorter events, 62.1 us)
Async XLA Ops:
  8.8 144.1 %all-to-all-start = ((f32[20,64,1024]{2,0,1:T(8,128)}), f32[20,64,1024]{2,0,1:T(8,128)}, u32[]{:S(2)}, u32[]{:S(2)}) async-start(f32[20,64,1024]{2,0,1:T(8,128)} %copy.187), calls=%async_computation | async-start | bytes 12582912 | tf_op jit(solution)/shard_map/all_to_all | solution.py:81
  182.9 8.7 %copy-start.2 = (f32[320,64,64]{0,1,2:T(8,128)S(1)}, f32[320,64,64]{0,1,2:T(8,128)}, u32[]{:S(2)}) copy-start(f32[320,64,64]{0,1,2:T(8,128)} %copy.191) | copy-start | bytes 15728644
  199.2 27.2 %copy-start.1 = (f32[320,64,64]{0,1,2:T(8,128)}, f32[320,64,64]{0,1,2:T(8,128)S(1)}, u32[]{:S(2)}) copy-start(f32[320,64,64]{0,1,2:T(8,128)S(1)} %get-tuple-element.17) | copy-start | bytes 15728644
  258.9 10.3 %copy-start = (f32[320,64,64]{0,2,1:T(8,128)S(1)}, f32[320,64,64]{0,2,1:T(8,128)}, u32[]{:S(2)}) copy-start(f32[320,64,64]{0,2,1:T(8,128)} %get-tuple-element.14) | copy-start | bytes 15728644
  300.1 12.4 %copy-start.3 = (f32[320,64,64]{0,2,1:T(8,128)S(1)}, f32[320,64,64]{0,2,1:T(8,128)}, u32[]{:S(2)}) copy-start(f32[320,64,64]{0,2,1:T(8,128)} %get-tuple-element.12) | copy-start | bytes 15728644
  420.9 5.2 copy-start.4
  420.9 120.3 %all-to-all-start.1 = ((f32[4,1,327680]{2,1,0:T(1,128)}), f32[4,1,327680]{2,1,0:T(1,128)}, u32[]{:S(2)}, u32[]{:S(2)}) async-start(f32[4,1,327680]{2,1,0:T(1,128)} %reshape.131), calls=%async_computation.1 | async-start | bytes 10485760 | tf_op jit(solution)/shard_map/all_to_all | solution.py:83
  426.5 12.6 %copy-start.6 = (s32[32,2]{0,1:T(2,128)S(1)}, s32[32,2]{0,1:T(2,128)}, u32[]{:S(2)}) copy-start(s32[32,2]{0,1:T(2,128)} %param.9) | copy-start | bytes 772
  427.5 233.4 %collective-permute-start.3 = (f32[5,32,1,1024]{3,1,0,2:T(8,128)}, f32[5,32,1,1024]{3,1,0,2:T(8,128)}, u32[]{:S(2)}, u32[]{:S(2)}) collective-permute-start(f32[5,32,1,1024]{3,1,0,2:T(8,128)} %get-tuple-element.30), channel_id=1, source_target_pairs={{0,1},{1,2},{2,3},{4,5},{5,6},{6,7},{8,9},{9,10},{10,11},{12,13},{... | collective-permute-start | bytes 1966088 | tf_op jit(solution)/shard_map/ppermute | solution.py:21
  431.8 230.3 %collective-permute-start.2 = (f32[5,32,1,1024]{3,1,0,2:T(8,128)S(1)}, f32[5,32,1,1024]{3,1,0,2:T(8,128)}, u32[]{:S(2)}, u32[]{:S(2)}) collective-permute-start(f32[5,32,1,1024]{3,1,0,2:T(8,128)S(1)} %get-tuple-element.31), channel_id=1, source_target_pairs={{1,0},{2,1},{3,2},{5,4},{6,5},{7,6},{9,8},{10,9},{11,10},{13,12},{... | collective-permute-start | bytes 1966088 | tf_op jit(solution)/shard_map/ppermute | solution.py:22
  433.8 228.3 %collective-permute-start = (f32[5,1,2,1024]{3,1,0,2:T(1,128)S(1)}, f32[5,1,2,1024]{3,1,0,2:T(1,128)S(1)}, u32[]{:S(2)}, u32[]{:S(2)}) collective-permute-start(f32[5,1,2,1024]{3,1,0,2:T(1,128)S(1)} %copy.181), channel_id=1, source_target_pairs={{4,0},{5,1},{6,2},{7,3},{12,8},{13,9},{14,10},{15,11},{20,16},{21,... | collective-permute-start | bytes 122888 | tf_op jit(solution)/shard_map/ppermute | solution.py:22
  435.1 227.0 %collective-permute-start.1 = (f32[5,1,2,1024]{3,1,0,2:T(1,128)S(1)}, f32[5,1,2,1024]{3,1,0,2:T(1,128)S(1)}, u32[]{:S(2)}, u32[]{:S(2)}) collective-permute-start(f32[5,1,2,1024]{3,1,0,2:T(1,128)S(1)} %copy.183), channel_id=1, source_target_pairs={{0,4},{1,5},{2,6},{3,7},{8,12},{9,13},{10,14},{11,15},{16,20},{17,... | collective-permute-start | bytes 122888 | tf_op jit(solution)/shard_map/ppermute | solution.py:21
  644.6 4.6 copy-start.7
  651.9 10.2 %copy-start.5 = (f32[5]{0:T(128)S(1)}, f32[5]{0:T(128)}, u32[]{:S(2)}) copy-start(f32[5]{0:T(128)} %constant.78) | copy-start | bytes 64
  664.2 9.9 %collective-permute-start.7 = (f32[5,32,1,1024]{3,1,0,2:T(8,128)S(1)}, f32[5,32,1,1024]{3,1,0,2:T(8,128)S(1)}, u32[]{:S(2)}, u32[]{:S(2)}) collective-permute-start(f32[5,32,1,1024]{3,1,0,2:T(8,128)S(1)} %get-tuple-element.28), channel_id=1, source_target_pairs={{0,1},{1,2},{2,3},{4,5},{5,6},{6,7},{8,9},{9,10},{10,11},{12,13},{... | collective-permute-start | bytes 1966088 | tf_op jit(solution)/shard_map/ppermute | solution.py:21
  666.7 11.9 %collective-permute-start.6 = (f32[5,32,1,1024]{3,1,0,2:T(8,128)S(1)}, f32[5,32,1,1024]{3,1,0,2:T(8,128)S(1)}, u32[]{:S(2)}, u32[]{:S(2)}) collective-permute-start(f32[5,32,1,1024]{3,1,0,2:T(8,128)S(1)} %get-tuple-element.29), channel_id=1, source_target_pairs={{1,0},{2,1},{3,2},{5,4},{6,5},{7,6},{9,8},{10,9},{11,10},{13,12},{... | collective-permute-start | bytes 1966088 | tf_op jit(solution)/shard_map/ppermute | solution.py:22
  668.7 5.6 collective-permute-start.4
  670.0 5.2 collective-permute-start.5
  679.8 10.0 %collective-permute-start.11 = (f32[5,32,1,1024]{3,1,0,2:T(8,128)S(1)}, f32[5,32,1,1024]{3,1,0,2:T(8,128)S(1)}, u32[]{:S(2)}, u32[]{:S(2)}) collective-permute-start(f32[5,32,1,1024]{3,1,0,2:T(8,128)S(1)} %get-tuple-element.24), channel_id=1, source_target_pairs={{0,1},{1,2},{2,3},{4,5},{5,6},{6,7},{8,9},{9,10},{10,11},{12,13},{... | collective-permute-start | bytes 1966088 | tf_op jit(solution)/shard_map/ppermute | solution.py:21
  681.7 11.9 %collective-permute-start.10 = (f32[5,32,1,1024]{3,1,0,2:T(8,128)S(1)}, f32[5,32,1,1024]{3,1,0,2:T(8,128)S(1)}, u32[]{:S(2)}, u32[]{:S(2)}) collective-permute-start(f32[5,32,1,1024]{3,1,0,2:T(8,128)S(1)} %get-tuple-element.25), channel_id=1, source_target_pairs={{1,0},{2,1},{3,2},{5,4},{6,5},{7,6},{9,8},{10,9},{11,10},{13,12},{... | collective-permute-start | bytes 1966088 | tf_op jit(solution)/shard_map/ppermute | solution.py:22
  684.2 5.7 collective-permute-start.8
  685.5 5.2 collective-permute-start.9
  694.8 9.7 %collective-permute-start.15 = (f32[5,32,1,1024]{3,1,0,2:T(8,128)S(1)}, f32[5,32,1,1024]{3,1,0,2:T(8,128)S(1)}, u32[]{:S(2)}, u32[]{:S(2)}) collective-permute-start(f32[5,32,1,1024]{3,1,0,2:T(8,128)S(1)} %get-tuple-element.20), channel_id=1, source_target_pairs={{0,1},{1,2},{2,3},{4,5},{5,6},{6,7},{8,9},{9,10},{10,11},{12,13},{... | collective-permute-start | bytes 1966088 | tf_op jit(solution)/shard_map/ppermute | solution.py:21
  696.7 11.9 %collective-permute-start.14 = (f32[5,32,1,1024]{3,1,0,2:T(8,128)S(1)}, f32[5,32,1,1024]{3,1,0,2:T(8,128)S(1)}, u32[]{:S(2)}, u32[]{:S(2)}) collective-permute-start(f32[5,32,1,1024]{3,1,0,2:T(8,128)S(1)} %get-tuple-element.21), channel_id=1, source_target_pairs={{1,0},{2,1},{3,2},{5,4},{6,5},{7,6},{9,8},{10,9},{11,10},{13,12},{... | collective-permute-start | bytes 1966088 | tf_op jit(solution)/shard_map/ppermute | solution.py:22
  699.2 5.4 collective-permute-start.12
  700.5 5.2 collective-permute-start.13
where the time goes:
time: 722 us; the launch traced here: 716 us
  waiting for transfers between devices  252 us (35%)
  local copies, waits for them, and re-layouts  225 us (31%)
  matrix products  143 us (20%)
  starting transfers between devices  51.5 us (7%)
  other arithmetic  34.3 us (5%)
  blocking collectives  8.99 us (1%)
    all_to_all x1, waiting for transfers between devices, on_device(): lax.all_to_all(stacked, 'az', split_axis=1, concat_axis=2, tiled=True)  137 us
    unnamed x20, local copies, waits for them, and re-layouts  112 us
    all_to_all x1, waiting for transfers between devices, on_device(): lax.all_to_all(moved, 'az', split_axis=2, concat_axis=1, tiled=True)  102 us
    all_to_all x3, local copies, waits for them, and re-layouts, on_device(): lax.all_to_all(moved, 'az', split_axis=2, concat_axis=1, tiled=True)  32.1 us
    another operation x2, local copies, waits for them, and re-layouts, on_device(): spectral_shift(piece.reshape(-1, piece.shape[2]), shift_value)  28.5 us
    ppermute x8, starting transfers between devices, padded(): before = lax.ppermute(last, axis, up)  26.7 us
    another operation x2, local copies, waits for them, and re-layouts, spectral_shift(): grid = rows.reshape(count, outer, inner)  21.5 us
    dot_general x1, matrix products, spectral_shift(): jnp.einsum('bkq,qm->bkm', twist_im, cos_inner, precision=hp)  19.1 us
  transfers between devices with their start and end apart: 18, of which 9 were waited for; matrix products, arithmetic and copies ran while one was open for 16% of the time, Pallas kernels for 0%

commit v1 on v0

--- a/solution.py
+++ b/solution.py
@@ -1,3 +1,4 @@
+import functools
 import math
 import jax
 import jax.numpy as jnp
@@ -9,6 +10,29 @@
 AXIAL_SPEEDS = (0.35, 0.2, 0.3, 0.25, 0.4)
 DIFFUSION = 0.15
 SWIRL_SPEED = 0.1
+
+
+def column_obtain(local_block, in_dim, d_out):
+    plain, n_now = (lax.axis_size("az"), lax.axis_index("az"))
+    z_new = local_block.shape[in_dim] // plain
+    raw_out = list(local_block.shape)
+    raw_out[in_dim] = z_new
+    carry_in = raw_out[d_out]
+    raw_out[d_out] = carry_in * plain
+    value_now = jnp.zeros(raw_out, local_block.dtype)
+    for p in range(plain):
+        h_now = lax.dynamic_slice_in_dim(local_block, (n_now ^ p) * z_new, z_new, axis=in_dim)
+        if p:
+            h_now = lax.ppermute(
+                h_now, axis_name="az", perm=[(dev_i, dev_i ^ p) for dev_i in range(plain)]
+            )
+        value_now = lax.dynamic_update_slice_in_dim(
+            value_now, h_now, (n_now ^ p) * carry_in, axis=d_out
+        )
+    return value_now
+
+
+manage_notes = functools.partial(column_obtain, in_dim=2, d_out=1)
 
 
 def padded(array, sides, width):
@@ -80,7 +104,7 @@
     shift_value = shift[0]
     piece = lax.all_to_all(stacked, "az", split_axis=1, concat_axis=2, tiled=True)
     moved = spectral_shift(piece.reshape(-1, piece.shape[2]), shift_value).reshape(piece.shape)
-    shifted_flat = lax.all_to_all(moved, "az", split_axis=2, concat_axis=1, tiled=True)
+    shifted_flat = manage_notes(moved)
     shifted_cycle = shifted_flat.reshape(layers, variables, radial, sector)
     weights = jnp.array(LAYER_WEIGHTS, jnp.float32)
     depth, count, rows, width = shifted_cycle.shape

time: 722 us -> 547 us (0.76)
  the two profiles are of different devices: /device:TPU:1 before, /device:TPU:9 now
where the time goes in v1:
time: 547 us; the launch traced here: 542 us
  waiting for transfers between devices  215 us (39%)
  matrix products  143 us (26%)
  local copies, waits for them, and re-layouts  79.3 us (14%)
  starting transfers between devices  76.1 us (14%)
  other arithmetic  15.9 us (3%)
  blocking collectives  9.72 us (2%)
    all_to_all x1, waiting for transfers between devices, on_device(): lax.all_to_all(stacked, 'az', split_axis=1, concat_axis=2, tiled=True)  134 us
    ppermute x3, waiting for transfers between devices, column_obtain(): lax.ppermute(h_now, axis_name='az', perm=[(dev_i, dev_i ^ p) for dev_i in...  66.7 us
    ppermute x8, starting transfers between devices, padded(): before = lax.ppermute(last, axis, up)  50.6 us
    another operation x2, local copies, waits for them, and re-layouts, spectral_shift(): grid = rows.reshape(count, outer, inner)  21.4 us
    dot_general x1, matrix products, spectral_shift(): jnp.einsum('bkq,qm->bkm', twist_im, cos_inner, precision=hp)  19.1 us
    ppermute x8, starting transfers between devices, padded(): after = lax.ppermute(leading, axis, down)  15.2 us
    dot_general x1, matrix products, spectral_shift(): jnp.einsum('bkm,qm->bkq', mixed_im, cos_inner, precision=hp)  15 us
    dot_general x1, matrix products, spectral_shift(): jnp.einsum('bkq,qm->bkm', twist_re, sin_inner, precision=hp)  13.8 us
  transfers between devices with their start and end apart: 20, of which 11 were waited for; matrix products, arithmetic and copies ran while one was open for 3% of the time, Pallas kernels for 0%

profile of v1, /device:TPU:9, one launch (start us, length us, event | category | flops | bytes accessed | tf_op | source)
XLA Modules:
  0.0 541.9 jit_solution(9781264295532800191)
XLA Ops:
  0.6 8.2 %copy.144 = f32[20,64,1024]{2,0,1:T(8,128)} copy(f32[20,64,1024]{2,1,0:T(8,128)} %bitcast.88) | data formatting | bytes 10485760 | tf_op jit(solution)/shard_map/reshape | solution.py:103
  8.9 5.8 %all-to-all-start = ((f32[20,64,1024]{2,0,1:T(8,128)}), f32[20,64,1024]{2,0,1:T(8,128)}, u32[]{:S(2)}, u32[]{:S(2)}) async-start(f32[20,64,1024]{2,0,1:T(8,128)} %copy.144), calls=%async_computation | async-start | bytes 12582912 | tf_op jit(solution)/shard_map/all_to_all | solution.py:105
  15.8 133.5 %all-to-all-done = f32[20,64,1024]{2,0,1:T(8,128)} async-done(((f32[20,64,1024]{2,0,1:T(8,128)}), f32[20,64,1024]{2,0,1:T(8,128)}, u32[]{:S(2)}, u32[]{:S(2)}) %all-to-all-start) | async-done | bytes 5242912 | tf_op jit(solution)/shard_map/all_to_all | solution.py:105
  149.3 8.5 %copy.146 = f32[20,16,4,1024]{3,2,1,0:T(4,128)} copy(f32[20,16,4,1024]{3,0,1,2:T(8,128)} %bitcast.5) | data formatting | bytes 10485760 | tf_op jit(solution)/shard_map/all_to_all | solution.py:105
  157.8 9.6 %reshape_reshape.9 = f32[320,64,64]{2,1,0:T(8,128)} reshape(f32[20,16,4,1024]{3,2,1,0:T(4,128)} %copy.146) | data formatting | bytes 10485760 | tf_op jit(solution)/shard_map/reshape;reshape | solution.py:68
  167.4 11.8 %copy.148 = f32[320,64,64]{0,1,2:T(8,128)} copy(f32[320,64,64]{2,1,0:T(8,128)} %reshape_reshape.9) | data formatting | bytes 10485760 | tf_op jit(solution)/shard_map/reshape;reshape | solution.py:68
  179.2 8.7 %fusion.44 = f32[64,320,64]{1,0,2:T(8,128)S(1)} fusion(f32[320,64,64]{0,1,2:T(8,128)} %copy.148), kind=kOutput, calls=%fused_computation.86 | convolution fusion | flops 1006690304 | bytes 10485760 | tf_op jit(solution)/shard_map/bpq,pk->bkq/dot_general | solution.py:70
  187.9 7.6 %add_bitcast_fusion = (f32[320,64,64]{0,1,2:T(8,128)S(1)}, f32[320,64,64]{0,1,2:T(8,128)S(1)}) fusion(f32[64,320,64]{1,0,2:T(8,128)S(1)} %fusion.44, f32[64,64]{0,1:T(8,128)S(1)} %copy.152, f32[64,64]{0,1:T(8,128)S(1)} %copy.149, f32[320,64,64]{0,1,2:T(8,128)S(1)} %copy-done.2), kind=kOutput, calls=%fused_computation.10 | convolution fusion | flops 1015865344 | bytes 21004288 | tf_op jit(solution)/shard_map/bpq,pk->bkq/dot_general | solution.py:69
  195.6 13.8 %fusion.8 = f32[320,64,64]{0,2,1:T(8,128)} fusion(f32[320,64,64]{0,1,2:T(8,128)S(1)} %get-tuple-element.14), kind=kOutput, calls=%fused_computation.15 | convolution fusion | flops 1006690304 | bytes 10485760 | tf_op jit(solution)/shard_map/bkq,qm->bkm/dot_general | solution.py:76
  209.4 13.2 %fusion.10 = f32[320,64,64]{0,2,1:T(8,128)} fusion(f32[320,64,64]{0,1,2:T(8,128)S(1)} %get-tuple-element.14), kind=kOutput, calls=%fused_computation.17 | convolution fusion | flops 1006690304 | bytes 10485760 | tf_op jit(solution)/shard_map/bkq,qm->bkm/dot_general | solution.py:73
  222.6 13.5 %fusion.6 = f32[320,64,64]{0,2,1:T(8,128)} fusion(f32[320,64,64]{0,1,2:T(8,128)S(1)} %get-tuple-element.15), kind=kOutput, calls=%fused_computation.13 | convolution fusion | flops 1006690304 | bytes 10485760 | tf_op jit(solution)/shard_map/bkq,qm->bkm/dot_general | solution.py:73
  236.1 19.1 %multiply_subtract_fusion.1 = (f32[320,64,64]{0,2,1:T(8,128)}, f32[320,64,64]{0,2,1:T(8,128)S(1)}) fusion(f32[64,64]{1,0:T(8,128)S(1)} %get-tuple-element.37, f32[64,64]{1,0:T(8,128)S(1)} %get-tuple-element.36, f32[320,64,64]{0,2,1:T(8,128)} %fusion.8, f32[320,64,64]{0,2,1:T(8,128)} %fusion.10, f32[320,64,64]{0,2,1:T(8,128)} %fusion.6, ...), kind=kOutput, calls=%fused_computation.8 | convolution fusion | flops 1017176064 | bytes 31490048 | tf_op jit(solution)/shard_map/bkq,qm->bkm/dot_general | solution.py:76
  255.3 10.2 %fusion.38 = f32[320,64,64]{0,2,1:T(8,128)} fusion(f32[320,64,64]{0,2,1:T(8,128)} %get-tuple-element.12), kind=kOutput, calls=%fused_computation.80 | convolution fusion | flops 1006690304 | bytes 10485760 | tf_op jit(solution)/shard_map/bkm,qm->bkq/dot_general | solution.py:90
  265.5 7.8 %fusion.53 = f32[320,64,64]{0,2,1:T(8,128)} fusion(f32[320,64,64]{0,2,1:T(8,128)S(1)} %copy-done), kind=kOutput, calls=%fused_computation.95 | convolution fusion | flops 1006690304 | bytes 10485760 | tf_op jit(solution)/shard_map/bkm,qm->bkq/dot_general | solution.py:87
  273.3 7.9 %fusion.40 = f32[320,64,64]{0,2,1:T(8,128)} fusion(f32[320,64,64]{0,2,1:T(8,128)S(1)} %get-tuple-element.13), kind=kOutput, calls=%fused_computation.82 | convolution fusion | flops 1006690304 | bytes 10485760 | tf_op jit(solution)/shard_map/bkm,qm->bkq/dot_general | solution.py:87
  281.2 15.0 %multiply_subtract_fusion = (f32[320,64,64]{0,2,1:T(8,128)}, f32[320,64,64]{0,2,1:T(8,128)}) fusion(f32[64,64]{1,0:T(8,128)S(1)} %get-tuple-element.38, f32[64,64]{1,0:T(8,128)S(1)} %get-tuple-element.39, f32[320,64,64]{0,2,1:T(8,128)} %fusion.38, f32[320,64,64]{0,2,1:T(8,128)} %fusion.53, f32[320,64,64]{0,2,1:T(8,128)} %fusion.40, ...), kind=kOutput, calls=%fused_computation.6 | convolution fusion | flops 1017176064 | bytes 31490048 | tf_op jit(solution)/shard_map/bkm,qm->bkq/dot_general | solution.py:90
  296.2 12.4 %fusion = f32[64,320,64]{1,0,2:T(8,128)S(1)} fusion(f32[320,64,64]{0,2,1:T(8,128)} %get-tuple-element.11), kind=kOutput, calls=%fused_computation | convolution fusion | flops 1006690304 | bytes 10485760 | tf_op jit(solution)/shard_map/bkq,pk->bpq/dot_general | solution.py:95
  308.6 11.5 %multiply_bitcast_fusion = f32[320,64,64]{0,1,2:T(8,128)} fusion(f32[64,320,64]{1,0,2:T(8,128)S(1)} %fusion, f32[320,64,64]{0,2,1:T(8,128)S(1)} %copy-done.3), kind=kOutput, calls=%fused_computation.4 | convolution fusion | flops 1009311744 | bytes 15728640 | tf_op jit(solution)/shard_map/bkq,pk->bpq/dot_general | solution.py:95
  320.1 12.5 %copy.163 = f32[320,64,64]{2,1,0:T(8,128)} copy(f32[320,64,64]{0,1,2:T(8,128)} %multiply_bitcast_fusion) | data formatting | bytes 10485760 | tf_op jit(solution)/shard_map/div | solution.py:98
  332.6 9.7 %reshape_reshape.10 = f32[20,16,4096]{2,1,0:T(8,128)} reshape(f32[320,64,64]{2,1,0:T(8,128)} %copy.163) | data formatting | bytes 10485760 | tf_op jit(solution)/shard_map/reshape;reshape | solution.py:106
  342.3 3.3 broadcast_in_dim.10
  349.3 3.3 collective-permute-start.3
  355.2 4.0 collective-permute-start.1
  360.6 46.4 %collective-permute-done.3 = f32[20,16,1024]{2,1,0:T(8,128)} collective-permute-done((f32[20,16,1024]{2,1,0:T(8,128)}, f32[20,16,1024]{2,1,0:T(8,128)}, u32[]{:S(2)}, u32[]{:S(2)}) %collective-permute-start.3) | collective-permute-done | bytes 1310752 | tf_op jit(solution)/shard_map/ppermute | solution.py:26
  407.0 3.6 collective-permute-start.2
  413.2 29.9 %collective-permute-start.6 = (f32[5,32,1,1024]{3,1,0,2:T(8,128)}, f32[5,32,1,1024]{3,1,0,2:T(8,128)}, u32[]{:S(2)}, u32[]{:S(2)}) collective-permute-start(f32[5,32,1,1024]{3,1,0,2:T(8,128)} %get-tuple-element.32), channel_id=1, source_target_pairs={{0,1},{1,2},{2,3},{4,5},{5,6},{6,7},{8,9},{9,10},{10,11},{12,13},{... | collective-permute-start | bytes 1966088 | tf_op jit(solution)/shard_map/ppermute | solution.py:45
  445.6 20.4 %collective-permute-done.5 = f32[20,16,1024]{2,1,0:T(8,128)} collective-permute-done((f32[20,16,1024]{2,1,0:T(8,128)}, f32[20,16,1024]{2,1,0:T(8,128)}, u32[]{:S(2)}, u32[]{:S(2)}) %collective-permute-start.5) | collective-permute-done | bytes 1310752 | tf_op jit(solution)/shard_map/ppermute | solution.py:26
  468.5 4.6 reduce_sum.9
  475.8 9.7 %all_gather.3 = f32[5,32,1024]{2,1,0:T(8,128)S(1)} all-gather(f32[5,8,1024]{2,1,0:T(8,128)S(1)} %bitcast_multiply_fusion), channel_id=1, replica_groups=mesh['az'=4,'rad'=2,'ax'=4] {'ax'}, dimensions={1}, use_global_device_ids=true | all-gather | bytes 819200 | tf_op jit(solution)/shard_map/all_gather | solution.py:112
  493.3 3.1 collective-permute-start.8
  526.1 4.0 collective-permute-start.16
  534.1 5.5 %multiply_add_fusion.2 = f32[5,32,2,1024]{3,1,0,2:T(8,128)S(1)} fusion(f32[5,32,2,1024]{3,1,0,2:T(8,128)S(1)} %copy.169, f32[5,32,2,1024]{3,1,0,2:T(8,128)S(1)} %copy_add_fusion, f32[5,32,1,1024]{3,1,0,2:T(8,128)S(1)} %get-tuple-element.23, f32[5,32,1,1024]{3,1,0,2:T(8,128)S(1)} %fusion.22, f32[5,32,1,1024]{3,1,0,2:T(8,128)S(1)} %collective-permute-done.17, ...), kind=kLoop, calls=%fused_computation.35 | loop fusion | flops 24576000 | bytes 14745876 | tf_op jit(solution)/shard_map/add | solution.py:140
  (79 shorter events, 61.8 us)
Async XLA Ops:
  8.9 140.4 %all-to-all-start = ((f32[20,64,1024]{2,0,1:T(8,128)}), f32[20,64,1024]{2,0,1:T(8,128)}, u32[]{:S(2)}, u32[]{:S(2)}) async-start(f32[20,64,1024]{2,0,1:T(8,128)} %copy.144), calls=%async_computation | async-start | bytes 12582912 | tf_op jit(solution)/shard_map/all_to_all | solution.py:105
  179.2 8.7 %copy-start.2 = (f32[320,64,64]{0,1,2:T(8,128)S(1)}, f32[320,64,64]{0,1,2:T(8,128)}, u32[]{:S(2)}) copy-start(f32[320,64,64]{0,1,2:T(8,128)} %copy.148) | copy-start | bytes 15728644
  195.5 27.0 %copy-start.1 = (f32[320,64,64]{0,1,2:T(8,128)}, f32[320,64,64]{0,1,2:T(8,128)S(1)}, u32[]{:S(2)}) copy-start(f32[320,64,64]{0,1,2:T(8,128)S(1)} %get-tuple-element.15) | copy-start | bytes 15728644
  255.2 10.3 %copy-start = (f32[320,64,64]{0,2,1:T(8,128)S(1)}, f32[320,64,64]{0,2,1:T(8,128)}, u32[]{:S(2)}) copy-start(f32[320,64,64]{0,2,1:T(8,128)} %get-tuple-element.12) | copy-start | bytes 15728644
  296.2 12.4 %copy-start.3 = (f32[320,64,64]{0,2,1:T(8,128)S(1)}, f32[320,64,64]{0,2,1:T(8,128)}, u32[]{:S(2)}) copy-start(f32[320,64,64]{0,2,1:T(8,128)} %get-tuple-element.10) | copy-start | bytes 15728644
  342.3 4.4 copy-start.4
  346.7 7.1 %copy-start.5 = (f32[5,32,2,1024]{3,2,1,0:T(2,128)S(1)}, f32[5,32,2,1024]{3,2,1,0:T(2,128)}, u32[]{:S(2)}) copy-start(f32[5,32,2,1024]{3,2,1,0:T(2,128)} %param.7) | copy-start | bytes 3932164
  349.3 57.7 %collective-permute-start.3 = (f32[20,16,1024]{2,1,0:T(8,128)}, f32[20,16,1024]{2,1,0:T(8,128)}, u32[]{:S(2)}, u32[]{:S(2)}) collective-permute-start(f32[20,16,1024]{2,1,0:T(8,128)} %get-tuple-element.18), channel_id=1, source_target_pairs={{0,8},{8,0},{16,24},{24,16},{1,9},{9,1},{17,25},{25,17},{2,10},{10... | collective-permute-start | bytes 3932168 | tf_op jit(solution)/shard_map/ppermute | solution.py:26
  352.6 60.6 %collective-permute-start.4 = (f32[20,16,1024]{2,1,0:T(8,128)}, f32[20,16,1024]{2,1,0:T(8,128)}, u32[]{:S(2)}, u32[]{:S(2)}) collective-permute-start(f32[20,16,1024]{2,1,0:T(8,128)} %get-tuple-element.17), channel_id=1, source_target_pairs={{0,16},{8,24},{16,0},{24,8},{1,17},{9,25},{17,1},{25,9},{2,18},{10... | collective-permute-start | bytes 3932168 | tf_op jit(solution)/shard_map/ppermute | solution.py:26
  352.6 113.4 %collective-permute-start.5 = (f32[20,16,1024]{2,1,0:T(8,128)}, f32[20,16,1024]{2,1,0:T(8,128)}, u32[]{:S(2)}, u32[]{:S(2)}) collective-permute-start(f32[20,16,1024]{2,1,0:T(8,128)} %get-tuple-element.16), channel_id=1, source_target_pairs={{0,24},{8,16},{16,8},{24,0},{1,25},{9,17},{17,9},{25,1},{2,26},{10... | collective-permute-start | bytes 3932168 | tf_op jit(solution)/shard_map/ppermute | solution.py:26
  353.8 132.9 %collective-permute-start = (f32[5,1,2,1024]{3,1,0,2:T(1,128)S(1)}, f32[5,1,2,1024]{3,1,0,2:T(1,128)S(1)}, u32[]{:S(2)}, u32[]{:S(2)}) collective-permute-start(f32[5,1,2,1024]{3,1,0,2:T(1,128)S(1)} %copy.138), channel_id=1, source_target_pairs={{4,0},{5,1},{6,2},{7,3},{12,8},{13,9},{14,10},{15,11},{20,16},{21,... | collective-permute-start | bytes 122888 | tf_op jit(solution)/shard_map/ppermute | solution.py:46
  355.2 4.5 copy-start.7
  355.2 131.6 %collective-permute-start.1 = (f32[5,1,2,1024]{3,1,0,2:T(1,128)S(1)}, f32[5,1,2,1024]{3,1,0,2:T(1,128)S(1)}, u32[]{:S(2)}, u32[]{:S(2)}) collective-permute-start(f32[5,1,2,1024]{3,1,0,2:T(1,128)S(1)} %copy.140), channel_id=1, source_target_pairs={{0,4},{1,5},{2,6},{3,7},{8,12},{9,13},{10,14},{11,15},{16,20},{17,... | collective-permute-start | bytes 122888 | tf_op jit(solution)/shard_map/ppermute | solution.py:45
  407.0 79.8 %collective-permute-start.2 = (f32[5,32,1,1024]{3,1,0,2:T(8,128)S(1)}, f32[5,32,1,1024]{3,1,0,2:T(8,128)}, u32[]{:S(2)}, u32[]{:S(2)}) collective-permute-start(f32[5,32,1,1024]{3,1,0,2:T(8,128)S(1)} %get-tuple-element.33), channel_id=1, source_target_pairs={{1,0},{2,1},{3,2},{5,4},{6,5},{7,6},{9,8},{10,9},{11,10},{13,12},{... | collective-permute-start | bytes 1966088 | tf_op jit(solution)/shard_map/ppermute | solution.py:46
  413.2 72.4 %collective-permute-start.6 = (f32[5,32,1,1024]{3,1,0,2:T(8,128)}, f32[5,32,1,1024]{3,1,0,2:T(8,128)}, u32[]{:S(2)}, u32[]{:S(2)}) collective-permute-start(f32[5,32,1,1024]{3,1,0,2:T(8,128)} %get-tuple-element.32), channel_id=1, source_target_pairs={{0,1},{1,2},{2,3},{4,5},{5,6},{6,7},{8,9},{9,10},{10,11},{12,13},{... | collective-permute-start | bytes 1966088 | tf_op jit(solution)/shard_map/ppermute | solution.py:45
  468.5 4.6 copy-start.8
  475.8 11.0 %copy-start.6 = (f32[5]{0:T(128)S(1)}, f32[5]{0:T(128)}, u32[]{:S(2)}) copy-start(f32[5]{0:T(128)} %constant.91) | copy-start | bytes 64
  488.9 9.9 %collective-permute-start.10 = (f32[5,32,1,1024]{3,1,0,2:T(8,128)S(1)}, f32[5,32,1,1024]{3,1,0,2:T(8,128)S(1)}, u32[]{:S(2)}, u32[]{:S(2)}) collective-permute-start(f32[5,32,1,1024]{3,1,0,2:T(8,128)S(1)} %get-tuple-element.30), channel_id=1, source_target_pairs={{0,1},{1,2},{2,3},{4,5},{5,6},{6,7},{8,9},{9,10},{10,11},{12,13},{... | collective-permute-start | bytes 1966088 | tf_op jit(solution)/shard_map/ppermute | solution.py:45
  491.3 11.9 %collective-permute-start.9 = (f32[5,32,1,1024]{3,1,0,2:T(8,128)S(1)}, f32[5,32,1,1024]{3,1,0,2:T(8,128)S(1)}, u32[]{:S(2)}, u32[]{:S(2)}) collective-permute-start(f32[5,32,1,1024]{3,1,0,2:T(8,128)S(1)} %get-tuple-element.31), channel_id=1, source_target_pairs={{1,0},{2,1},{3,2},{5,4},{6,5},{7,6},{9,8},{10,9},{11,10},{13,12},{... | collective-permute-start | bytes 1966088 | tf_op jit(solution)/shard_map/ppermute | solution.py:46
  493.3 5.5 %collective-permute-start.8 = (f32[5,1,2,1024]{3,1,0,2:T(1,128)S(1)}, f32[5,1,2,1024]{3,1,0,2:T(1,128)S(1)}, u32[]{:S(2)}, u32[]{:S(2)}) collective-permute-start(f32[5,1,2,1024]{3,1,0,2:T(1,128)S(1)} %get-tuple-element.29), channel_id=1, source_target_pairs={{0,4},{1,5},{2,6},{3,7},{8,12},{9,13},{10,14},{11,15},{16,20},{17,... | collective-permute-start | bytes 122888 | tf_op jit(solution)/shard_map/ppermute | solution.py:45
  496.4 5.4 collective-permute-start.7
  504.4 10.4 %collective-permute-start.14 = (f32[5,32,1,1024]{3,1,0,2:T(8,128)S(1)}, f32[5,32,1,1024]{3,1,0,2:T(8,128)S(1)}, u32[]{:S(2)}, u32[]{:S(2)}) collective-permute-start(f32[5,32,1,1024]{3,1,0,2:T(8,128)S(1)} %get-tuple-element.26), channel_id=1, source_target_pairs={{0,1},{1,2},{2,3},{4,5},{5,6},{6,7},{8,9},{9,10},{10,11},{12,13},{... | collective-permute-start | bytes 1966088 | tf_op jit(solution)/shard_map/ppermute | solution.py:45
  507.2 11.9 %collective-permute-start.13 = (f32[5,32,1,1024]{3,1,0,2:T(8,128)S(1)}, f32[5,32,1,1024]{3,1,0,2:T(8,128)S(1)}, u32[]{:S(2)}, u32[]{:S(2)}) collective-permute-start(f32[5,32,1,1024]{3,1,0,2:T(8,128)S(1)} %get-tuple-element.27), channel_id=1, source_target_pairs={{1,0},{2,1},{3,2},{5,4},{6,5},{7,6},{9,8},{10,9},{11,10},{13,12},{... | collective-permute-start | bytes 1966088 | tf_op jit(solution)/shard_map/ppermute | solution.py:46
  509.2 5.6 %collective-permute-start.12 = (f32[5,1,2,1024]{3,1,0,2:T(1,128)S(1)}, f32[5,1,2,1024]{3,1,0,2:T(1,128)S(1)}, u32[]{:S(2)}, u32[]{:S(2)}) collective-permute-start(f32[5,1,2,1024]{3,1,0,2:T(1,128)S(1)} %get-tuple-element.25), channel_id=1, source_target_pairs={{0,4},{1,5},{2,6},{3,7},{8,12},{9,13},{10,14},{11,15},{16,20},{17,... | collective-permute-start | bytes 122888 | tf_op jit(solution)/shard_map/ppermute | solution.py:45
  511.8 5.4 collective-permute-start.11
  520.3 9.7 %collective-permute-start.18 = (f32[5,32,1,1024]{3,1,0,2:T(8,128)S(1)}, f32[5,32,1,1024]{3,1,0,2:T(8,128)S(1)}, u32[]{:S(2)}, u32[]{:S(2)}) collective-permute-start(f32[5,32,1,1024]{3,1,0,2:T(8,128)S(1)} %get-tuple-element.22), channel_id=1, source_target_pairs={{0,1},{1,2},{2,3},{4,5},{5,6},{6,7},{8,9},{9,10},{10,11},{12,13},{... | collective-permute-start | bytes 1966088 | tf_op jit(solution)/shard_map/ppermute | solution.py:45
  522.2 11.9 %collective-permute-start.17 = (f32[5,32,1,1024]{3,1,0,2:T(8,128)S(1)}, f32[5,32,1,1024]{3,1,0,2:T(8,128)S(1)}, u32[]{:S(2)}, u32[]{:S(2)}) collective-permute-start(f32[5,32,1,1024]{3,1,0,2:T(8,128)S(1)} %get-tuple-element.23), channel_id=1, source_target_pairs={{1,0},{2,1},{3,2},{5,4},{6,5},{7,6},{9,8},{10,9},{11,10},{13,12},{... | collective-permute-start | bytes 1966088 | tf_op jit(solution)/shard_map/ppermute | solution.py:46
  524.8 5.4 collective-permute-start.15
  526.1 5.2 collective-permute-start.16
